TPU v7x, 256 devices: a whole 4x4x8 slice. The times are simulated.
256 devices in a mesh: wide: 32 (over x, z), narrow: 8 (over y, core).
Axes of the slice: x: 4, y: 4, z: 8, core: 2. Of those that a mesh axis runs over, the one named last changes fastest.
Arguments:
- hidden_in: bfloat16 [16384, 1664], P(('wide', 'narrow')), may hold values from -3 to 3
- queries: bfloat16 [16, 1024, 1664], P('narrow', 'wide'), may hold values from -24 to 24
- keys: bfloat16 [16, 1024, 1664], P('narrow', 'wide'), may hold values from -24 to 24
- values: bfloat16 [16, 1024, 1664], P('narrow', 'wide'), may hold values from -12 to 12
- out_weight: bfloat16 [1664, 1664], P('narrow', 'wide'), may hold values from -0.25 to 0.25
- merge_weight: bfloat16 [4, 1664, 1664], P(None, 'narrow', 'wide'), may hold values from -0.125 to 0.125
- segment_ids: int32 [4096], P('wide'), may hold values from 0 to 15, never falling along the last dimension, each value on 1 to 2560 neighbouring positions
- owners: int32 [4096, 1], P('wide'), may hold values from 0 to 31; in each aligned block of 128 rows (0 to 127, 128 to 255, ...) at most 8 rows name the same one
Outputs:
- hidden_out: bfloat16 [16384, 1664], P(('wide', 'narrow'))
- delivered: bfloat16 [8192, 1664], P('wide', 'narrow')
Inputs may be any that keep to these rules, and one draw needn't show every extreme that they name: `segment_ids`: never falling along the tokens; the largest image or clip holds exactly 2560 merged tokens. `owners`: among the merged tokens of one index of wide, at most 8 share an owner, and exactly 8 do for some owner.
All inputs are finite; a program needn't handle non-finite values.
Results may differ from a plain program's by a relative error of at most 0.025.
Values may be sent and summed in bfloat16 or wider, within the bound.
A program may use at most 64 MiB of HBM per device.

v0:
```python
import math
import jax
import jax.numpy as jnp
from jax import lax
from jax.sharding import PartitionSpec as P

HEAD_DIM = 104
NEG = -1e30


def shards(hidden_in, queries, keys, values, out_weight, merge_weight, segment_ids, owners):
    heads_here, packed_rows, packed_width = queries.shape
    tok_rows = packed_rows * 16
    local_width = heads_here * HEAD_DIM
    scale = 1.0 / math.sqrt(HEAD_DIM)
    tok_seg = jnp.repeat(segment_ids, 4)
    seg_packed = tok_seg.reshape(1, packed_rows, 16)
    gathered_out, gathered_merge = (
        lax.all_gather(out_weight, "wide", axis=1, tiled=True),
        lax.all_gather(merge_weight, "wide", axis=2, tiled=True),
    )
    query_heads = queries.reshape(heads_here, tok_rows, HEAD_DIM)

    def key_block(carry, key_rows, value_rows, seg_rows):
        keep = tok_seg[:, None] == seg_rows[None, :]
        best, total, accum = carry
        key_heads = key_rows.reshape(heads_here, -1, HEAD_DIM)
        value_heads = value_rows.reshape(heads_here, -1, HEAD_DIM)
        scores = (
            jnp.einsum("hqd,hkd->hqk", query_heads, key_heads, preferred_element_type=jnp.float32)
            * scale
        )
        scores = jnp.where(keep[None], scores, NEG)
        new_best = jnp.maximum(best, jnp.max(scores, axis=-1))
        weights = jnp.where(keep[None], jnp.exp(scores - new_best[..., None]), 0.0)
        factor = jnp.exp(best - new_best)
        total = total * factor + jnp.sum(weights, axis=-1)
        accum = accum * factor[..., None] + jnp.einsum(
            "hqk,hkd->hqd",
            weights.astype(jnp.bfloat16),
            value_heads,
            preferred_element_type=jnp.float32,
        )
        return (new_best, total, accum)

    start_state = (
        jnp.full((heads_here, tok_rows), NEG, jnp.float32),
        jnp.zeros((heads_here, tok_rows), jnp.float32),
        jnp.zeros((heads_here, tok_rows, HEAD_DIM), jnp.float32),
    )
    carry = start_state
    key_rows = lax.all_gather(keys, "wide", axis=1, tiled=True)
    value_rows = lax.all_gather(values, "wide", axis=1, tiled=True)
    seg_rows = lax.all_gather(seg_packed, "wide", axis=1, tiled=True)
    count = key_rows.shape[1]
    blocks = count // 32
    stacked = (
        key_rows.reshape(heads_here, blocks, 32, packed_width).transpose(1, 0, 2, 3),
        value_rows.reshape(heads_here, blocks, 32, packed_width).transpose(1, 0, 2, 3),
        seg_rows.reshape(blocks, 512),
    )

    def step_block(state, item):
        return (key_block(state, item[0], item[1], item[2]), None)

    carry, unused = lax.scan(step_block, carry, stacked)
    best, total, accum = carry
    attn = (
        (accum / total[..., None])
        .transpose(1, 0, 2)
        .reshape(tok_rows, local_width)
        .astype(jnp.bfloat16)
    )
    partial_mix = jnp.dot(attn, gathered_out, preferred_element_type=jnp.float32)
    summed_mix = lax.psum_scatter(
        partial_mix.astype(jnp.bfloat16), "narrow", scatter_dimension=0, tiled=True
    ).astype(jnp.float32)
    hidden_out = (hidden_in.astype(jnp.float32) + summed_mix).astype(jnp.bfloat16)
    whole_rows = lax.all_gather(hidden_out, "narrow", axis=0, tiled=True)
    my_columns = lax.dynamic_slice_in_dim(
        whole_rows, lax.axis_index("narrow") * local_width, local_width, 1
    )
    merged_rows = tok_rows // 4
    grouped = my_columns.reshape(merged_rows, 4, local_width)
    partial_feat = jnp.einsum(
        "gjc,jco->go", grouped, gathered_merge, preferred_element_type=jnp.float32
    )
    feature = lax.psum_scatter(
        partial_feat.astype(jnp.bfloat16), "narrow", scatter_dimension=1, tiled=True
    )
    owner_count = lax.axis_size("wide")
    capacity = 2 * merged_rows // owner_count
    owner_col = owners[:, 0]
    onehot = (owner_col[:, None] == jnp.arange(owner_count, dtype=jnp.int32)[None, :]).astype(
        jnp.int32
    )
    rank = jnp.sum(jnp.cumsum(onehot, axis=0) * onehot, axis=1) - 1
    slot = owner_col * capacity + rank
    picker = (jnp.arange(owner_count * capacity, dtype=jnp.int32)[:, None] == slot[None, :]).astype(
        jnp.bfloat16
    )
    outgoing = jnp.dot(picker, feature, preferred_element_type=jnp.float32).astype(jnp.bfloat16)
    outgoing = outgoing.reshape(owner_count, capacity, feature.shape[1])
    arrived = lax.all_to_all(outgoing, "wide", split_axis=0, concat_axis=0, tiled=True)
    return (hidden_out, arrived.reshape(owner_count * capacity, feature.shape[1]))


def solution(mesh):
    return jax.shard_map(
        shards,
        mesh=mesh,
        in_specs=(
            P(("wide", "narrow"), None),
            P("narrow", "wide", None),
            P("narrow", "wide", None),
            P("narrow", "wide", None),
            P("narrow", "wide"),
            P(None, "narrow", "wide"),
            P("wide"),
            P("wide", None),
        ),
        out_specs=(P(("wide", "narrow"), None), P("wide", "narrow")),
        check_vma=False,
    )
```

profile of v0, /device:TPU:32, one launch (start us, length us, event | category | flops | bytes accessed | tf_op | source)
XLA Modules:
  0.0 576.4 jit_solution(16896971549550113275)
XLA Ops:
  9.7 51.9 %all_gather.18 = s32[1,1024,16]{2,0,1:T(1,128)S(1)} all-gather(s32[1,32,16]{2,0,1:T(1,128)S(1)} %copy.25), channel_id=1, replica_groups=mesh['wide'=32,'narrow'=8] {'wide'}, dimensions={1}, use_global_device_ids=true | all-gather | bytes 67584 | tf_op jit(solution)/shard_map/all_gather | solution.py:54
  62.1 2.0 reduce.3
  65.1 49.1 %all-gather = bf16[32,52,208]{2,1,0:T(8,128)(2,1)S(1)} all-gather(bf16[1,52,208]{2,1,0:T(8,128)(2,1)S(1)} %bitcast.77), channel_id=1, replica_groups=mesh['wide'=32,'narrow'=8] {'wide'}, dimensions={0}, use_global_device_ids=true | all-gather | bytes 713856 | tf_op jit(solution)/shard_map/all_gather | solution.py:19
  114.2 1.3 reshape.93
  115.5 82.9 %all-gather.8.cloned.1.call-done = bf16[2,1024,1664]{2,1,0:T(8,128)(2,1)} async-done(((bf16[2,32,1664]{2,1,0:T(8,128)(2,1)}), bf16[2,1024,1664]{2,1,0:T(8,128)(2,1)}) %all-gather.8.cloned.1.call-update) | async-done | bytes 6815760 | tf_op jit(solution)/shard_map/all_gather | solution.py:53
  198.4 167.4 %while.15 = (s32[]{:T(128)}, f32[2,512]{1,0:T(2,128)S(1)}, f32[2,512]{1,0:T(2,128)S(1)}, f32[2,512,104]{1,2,0:T(8,128)S(1)}, s32[32,512]{1,0:T(8,128)S(1)}, /*in...) while((s32[]{:T(128)}, f32[2,512]{1,0:T(2,128)S(1)}, ...), condition=%wide.region_3.4_spmd.clone, body=%wide.region_0.3_spmd.clone.sunk | while | flops 225506304 | bytes 10615425 | solution.py:66
  199.5 1.1 dynamic-slice_bitcast_fusion.3
  204.7 1.1 dynamic-slice_bitcast_fusion.3
  209.9 1.1 dynamic-slice_bitcast_fusion.3
  215.2 1.1 dynamic-slice_bitcast_fusion.3
  220.4 1.1 dynamic-slice_bitcast_fusion.3
  225.6 1.1 dynamic-slice_bitcast_fusion.3
  230.9 1.1 dynamic-slice_bitcast_fusion.3
  236.1 1.1 dynamic-slice_bitcast_fusion.3
  241.3 1.1 dynamic-slice_bitcast_fusion.3
  365.9 3.1 convolution_convert_fusion
  369.0 33.3 %reduce-scatter.5.cloned.1.call-done = bf16[64,1664]{1,0:T(8,128)(2,1)} async-done(((bf16[512,1664]{1,0:T(8,128)(2,1)}), bf16[64,1664]{1,0:T(8,128)(2,1)}) %reduce-scatter.5.cloned.1.call-update) | async-done | bytes 213008 | tf_op jit(solution)/shard_map/reduce_scatter | solution.py:75
  402.4 1.7 add_convert_fusion
  404.7 26.0 %all-gather.10.cloned.1.call-done = bf16[512,1664]{1,0:T(8,128)(2,1)} async-done(((bf16[64,1664]{1,0:T(8,128)(2,1)}), bf16[512,1664]{1,0:T(8,128)(2,1)}) %all-gather.10.cloned.1.call-update) | async-done | bytes 1703952 | tf_op jit(solution)/shard_map/all_gather | solution.py:79
  430.8 1.1 constant_dynamic-slice_fusion.1
  432.0 81.6 %all-gather.12.cloned.1.call-done = bf16[4,208,1664]{1,0,2:T(4,128)(2,1)} async-done(((bf16[4,208,52]{1,0,2:T(4,128)(2,1)}), bf16[4,208,1664]{1,0,2:T(4,128)(2,1)}) %all-gather.12.cloned.1.call-update) | async-done | bytes 2768912 | tf_op jit(solution)/shard_map/all_gather | solution.py:20
  513.6 3.8 fusion.23
  517.9 30.2 %reduce-scatter.7.cloned.1.call-done = bf16[208,128]{1,0:T(8,128)(2,1)} async-done(((bf16[1664,128]{1,0:T(8,128)(2,1)}), bf16[208,128]{1,0:T(8,128)(2,1)}) %reduce-scatter.7.cloned.1.call-update) | async-done | bytes 53264
  549.2 19.6 %all_to_all.5 = bf16[32,8,208]{2,1,0:T(8,128)(2,1)S(1)} all-to-all(bf16[32,8,208]{2,1,0:T(8,128)(2,1)S(1)} %bitcast.71), channel_id=1, replica_groups=mesh['wide'=32,'narrow'=8] {'wide'}, dimensions={0} | all-to-all | bytes 212992 | tf_op jit(solution)/shard_map/all_to_all | solution.py:104
  (448 shorter events, 161.8 us)
Async XLA Ops:
  7.2 57.2 %copy-start.1 = (bf16[2,32,1664]{2,1,0:T(8,128)(2,1)S(1)}, bf16[2,32,1664]{2,1,0:T(8,128)(2,1)}, u32[]{:S(2)}) copy-start(bf16[2,32,1664]{2,1,0:T(8,128)(2,1)} %param.11) | copy-start | bytes 638980
  7.2 57.9 %copy-start.2 = (bf16[208,52]{0,1:T(8,128)(2,1)S(1)}, bf16[208,52]{0,1:T(8,128)(2,1)}, u32[]{:S(2)}) copy-start(bf16[208,52]{0,1:T(8,128)(2,1)} %param.14) | copy-start | bytes 64900
  7.2 108.3 %all-gather.6.cloned.1.call-start = ((), (), s32[]{:S(2)}) async-start(), calls=%async_computation.3 | async-start | bytes 7028736 | tf_op jit(solution)/shard_map/all_gather | solution.py:52
  7.9 190.5 %all-gather.8.cloned.1.call-start = ((), (), s32[]{:S(2)}) async-start(), calls=%async_computation.4 | async-start | bytes 7028736 | tf_op jit(solution)/shard_map/all_gather | solution.py:53
  8.7 393.7 %reduce-scatter.5.cloned.1.call-start = ((), (), s32[]{:S(2)}) async-start(), calls=%async_computation.5 | async-start | bytes 1916928 | tf_op jit(solution)/shard_map/reduce_scatter | solution.py:75
  365.9 36.5 %copy-start = (bf16[64,1664]{1,0:T(8,128)(2,1)S(1)}, bf16[64,1664]{1,0:T(8,128)(2,1)}, u32[]{:S(2)}) copy-start(bf16[64,1664]{1,0:T(8,128)(2,1)} %param.10) | copy-start | bytes 638980
  369.0 61.8 %all-gather.10.cloned.1.call-start = ((), (), s32[]{:S(2)}) async-start(), calls=%async_computation.6 | async-start | bytes 1916928 | tf_op jit(solution)/shard_map/all_gather | solution.py:79
  404.1 109.6 %all-gather.12.cloned.1.call-start = ((), (), s32[]{:S(2)}) async-start(), calls=%async_computation.7 | async-start | bytes 3514368 | tf_op jit(solution)/shard_map/all_gather | solution.py:20
  404.7 143.5 %reduce-scatter.7.cloned.1.call-start = ((), (), s32[]{:S(2)}) async-start(), calls=%async_computation.8 | async-start | bytes 479232
  432.0 85.4 %copy-start.3 = (s32[128,1]{0,1:T(1,128)S(1)}, s32[128,1]{0,1:T(1,128)}, u32[]{:S(2)}) copy-start(s32[128,1]{0,1:T(1,128)} %param.17) | copy-start | bytes 1540
Sparse Core Ops, SparseCore 0:
  10.6 96.3 all-gather.5
  109.6 88.7 all-gather.7
  369.1 33.2 reduce-scatter.4
  404.8 25.9 all-gather.9
  433.5 80.0 all-gather.11
  517.5 30.5 reduce-scatter.6
where the time goes:
time: 578 us; the launch traced here: 576 us
  waiting for transfers between devices  256 us (44%)
  blocking collectives  121 us (21%)
  local copies, waits for them, and re-layouts  101 us (17%)
  matrix products  50.9 us (9%)
  other arithmetic  30.1 us (5%)
  between operations  14.3 us (2%)
    all_gather x1, waiting for transfers between devices, shards(): value_rows = lax.all_gather(values, 'wide', axis=1, tiled=True)  82.9 us
    all_gather x1, waiting for transfers between devices, shards(): lax.all_gather(merge_weight, 'wide', axis=2, tiled=True)  81.6 us
    all_gather x1, blocking collectives, shards(): seg_rows = lax.all_gather(seg_packed, 'wide', axis=1, tiled=True)  51.9 us
    all_gather x1, blocking collectives, shards(): lax.all_gather(out_weight, 'wide', axis=1, tiled=True)  49.1 us
    dynamic_slice x64, local copies, waits for them, and re-layouts, shards(): carry, unused = lax.scan(step_block, carry, stacked)  34.9 us
    reduce_scatter x1, waiting for transfers between devices, shards(): lax.psum_scatter(partial_mix.astype(jnp.bfloat16), 'narrow', scatter_dime...  33.3 us
    unnamed x7, waiting for transfers between devices  32.2 us
    all_gather x1, waiting for transfers between devices, shards(): whole_rows = lax.all_gather(hidden_out, 'narrow', axis=0, tiled=True)  26 us
  transfers between devices with their start and end apart: 6, of which 5 were waited for; matrix products, arithmetic and copies ran while one was open for 1% of the time, Pallas kernels for 0%

commit v1 on v0

--- a/solution.py
+++ b/solution.py
@@ -76,7 +76,13 @@
         partial_mix.astype(jnp.bfloat16), "narrow", scatter_dimension=0, tiled=True
     ).astype(jnp.float32)
     hidden_out = (hidden_in.astype(jnp.float32) + summed_mix).astype(jnp.bfloat16)
-    whole_rows = lax.all_gather(hidden_out, "narrow", axis=0, tiled=True)
+    devices = lax.axis_size("narrow")
+    held, tiles = (hidden_out, [hidden_out])
+    for _ in range(devices - 1):
+        held = lax.ppermute(held, "narrow", [(i, (i + 1) % devices) for i in range(devices)])
+        tiles.insert(0, held)
+    merged = jnp.concatenate(tiles, axis=0)
+    whole_rows = jnp.roll(merged, (lax.axis_index("narrow") + 1) * hidden_out.shape[0], axis=0)
     my_columns = lax.dynamic_slice_in_dim(
         whole_rows, lax.axis_index("narrow") * local_width, local_width, 1
     )

time: 578 us -> 547 us (0.946)
  waiting for transfers between devices: 256 us -> 227 us
    all_gather x1, waiting for transfers between devices: 81.6 us -> 34.3 us  [shards(): lax.all_gather(merge_weight, 'wide', axis=2, tiled=True)]
    ppermute x0 -> x7, waiting for transfers between devices: none -> 45.3 us  [shards(): lax.ppermute(held, 'narrow', [(i, (i + 1) % devices) for i in range(devic...]
    all_gather x1 -> x0, waiting for transfers between devices: 26 us -> none  [shards(): whole_rows = lax.all_gather(hidden_out, 'narrow', axis=0, tiled=True)]
    unnamed x7 -> x6, waiting for transfers between devices: 32.2 us -> 32.3 us
  transfers between devices with their start and end apart: 6 -> 12, of which waited for: 5 -> 11; matrix products, arithmetic and copies ran while one was open for 1% -> 2% of each run, Pallas kernels for 0% -> 0%
where the time goes in v1:
time: 547 us; the launch traced here: 546 us
  waiting for transfers between devices  227 us (41%)
  blocking collectives  120 us (22%)
  local copies, waits for them, and re-layouts  102 us (19%)
  matrix products  50.8 us (9%)
  other arithmetic  29.4 us (5%)
  between operations  14 us (3%)
    all_gather x1, waiting for transfers between devices, shards(): value_rows = lax.all_gather(values, 'wide', axis=1, tiled=True)  82.1 us
    all_gather x1, blocking collectives, shards(): seg_rows = lax.all_gather(seg_packed, 'wide', axis=1, tiled=True)  51.9 us
    all_gather x1, blocking collectives, shards(): lax.all_gather(out_weight, 'wide', axis=1, tiled=True)  48.9 us
    ppermute x7, waiting for transfers between devices, shards(): lax.ppermute(held, 'narrow', [(i, (i + 1) % devices) for i in range(devic...  45.3 us
    dynamic_slice x64, local copies, waits for them, and re-layouts, shards(): carry, unused = lax.scan(step_block, carry, stacked)  34.9 us
    all_gather x1, waiting for transfers between devices, shards(): lax.all_gather(merge_weight, 'wide', axis=2, tiled=True)  34.3 us
    reduce_scatter x1, waiting for transfers between devices, shards(): lax.psum_scatter(partial_mix.astype(jnp.bfloat16), 'narrow', scatter_dime...  32.8 us
    unnamed x6, waiting for transfers between devices  32.3 us
  transfers between devices with their start and end apart: 12, of which 11 were waited for; matrix products, arithmetic and copies ran while one was open for 2% of the time, Pallas kernels for 0%

profile of v1, /device:TPU:32, one launch (start us, length us, event | category | flops | bytes accessed | tf_op | source)
XLA Modules:
  0.0 546.1 jit_solution(9004640704300668794)
XLA Ops:
  9.7 51.9 %all_gather.15 = s32[1,1024,16]{2,0,1:T(1,128)S(1)} all-gather(s32[1,32,16]{2,0,1:T(1,128)S(1)} %copy.25), channel_id=1, replica_groups=mesh['wide'=32,'narrow'=8] {'wide'}, dimensions={1}, use_global_device_ids=true | all-gather | bytes 67584 | tf_op jit(solution)/shard_map/all_gather | solution.py:54
  62.1 2.0 reduce.3
  64.4 1.5 reshape.87
  66.0 48.9 %all-gather = bf16[32,52,208]{2,1,0:T(8,128)(2,1)S(1)} all-gather(bf16[1,52,208]{2,1,0:T(8,128)(2,1)S(1)} %bitcast.77), channel_id=1, replica_groups=mesh['wide'=32,'narrow'=8] {'wide'}, dimensions={0}, use_global_device_ids=true | all-gather | bytes 713856 | tf_op jit(solution)/shard_map/all_gather | solution.py:19
  114.9 1.3 reshape.93
  116.2 82.1 %all-gather.7.cloned.1.call-done = bf16[2,1024,1664]{2,1,0:T(8,128)(2,1)} async-done(((bf16[2,32,1664]{2,1,0:T(8,128)(2,1)}), bf16[2,1024,1664]{2,1,0:T(8,128)(2,1)}) %all-gather.7.cloned.1.call-update) | async-done | bytes 6815760 | tf_op jit(solution)/shard_map/all_gather | solution.py:53
  198.3 167.3 %while.15 = (s32[]{:T(128)}, f32[2,512]{1,0:T(2,128)S(1)}, f32[2,512]{1,0:T(2,128)S(1)}, f32[2,512,104]{1,2,0:T(8,128)S(1)}, s32[32,512]{1,0:T(8,128)S(1)}, /*in...) while((s32[]{:T(128)}, f32[2,512]{1,0:T(2,128)S(1)}, ...), condition=%wide.region_3.4_spmd.clone, body=%wide.region_0.3_spmd.clone.sunk | while | flops 225506304 | bytes 10615425 | solution.py:66
  199.4 1.1 dynamic-slice_bitcast_fusion.3
  204.6 1.1 dynamic-slice_bitcast_fusion.3
  209.9 1.1 dynamic-slice_bitcast_fusion.3
  215.1 1.1 dynamic-slice_bitcast_fusion.3
  365.7 3.1 convolution_convert_fusion
  369.5 32.8 %reduce-scatter.5.cloned.1.call-done = bf16[64,1664]{1,0:T(8,128)(2,1)} async-done(((bf16[512,1664]{1,0:T(8,128)(2,1)}), bf16[64,1664]{1,0:T(8,128)(2,1)}) %reduce-scatter.5.cloned.1.call-update) | async-done | bytes 213008 | tf_op jit(solution)/shard_map/reduce_scatter | solution.py:75
  403.3 6.5 %collective-permute-done = bf16[64,1664]{1,0:T(8,128)(2,1)S(1)} collective-permute-done((bf16[64,1664]{1,0:T(8,128)(2,1)S(1)}, bf16[64,1664]{1,0:T(8,128)(2,1)S(1)}, u32[]{:S(2)}, u32[]{:S(2)}) %collective-permute-start) | collective-permute-done | bytes 213024 | tf_op jit(solution)/shard_map/ppermute | solution.py:82
  409.7 6.5 %collective-permute-done.1 = bf16[64,1664]{1,0:T(8,128)(2,1)S(1)} collective-permute-done((bf16[64,1664]{1,0:T(8,128)(2,1)S(1)}, bf16[64,1664]{1,0:T(8,128)(2,1)S(1)}, u32[]{:S(2)}, u32[]{:S(2)}) %collective-permute-start.1) | collective-permute-done | bytes 213024 | tf_op jit(solution)/shard_map/ppermute | solution.py:82
  416.2 6.5 %collective-permute-done.2 = bf16[64,1664]{1,0:T(8,128)(2,1)S(1)} collective-permute-done((bf16[64,1664]{1,0:T(8,128)(2,1)S(1)}, bf16[64,1664]{1,0:T(8,128)(2,1)S(1)}, u32[]{:S(2)}, u32[]{:S(2)}) %collective-permute-start.2) | collective-permute-done | bytes 213024 | tf_op jit(solution)/shard_map/ppermute | solution.py:82
  422.7 6.5 %collective-permute-done.3 = bf16[64,1664]{1,0:T(8,128)(2,1)S(1)} collective-permute-done((bf16[64,1664]{1,0:T(8,128)(2,1)S(1)}, bf16[64,1664]{1,0:T(8,128)(2,1)S(1)}, u32[]{:S(2)}, u32[]{:S(2)}) %collective-permute-start.3) | collective-permute-done | bytes 213024 | tf_op jit(solution)/shard_map/ppermute | solution.py:82
  429.2 6.5 %collective-permute-done.4 = bf16[64,1664]{1,0:T(8,128)(2,1)S(1)} collective-permute-done((bf16[64,1664]{1,0:T(8,128)(2,1)S(1)}, bf16[64,1664]{1,0:T(8,128)(2,1)S(1)}, u32[]{:S(2)}, u32[]{:S(2)}) %collective-permute-start.4) | collective-permute-done | bytes 213024 | tf_op jit(solution)/shard_map/ppermute | solution.py:82
  435.7 6.5 %collective-permute-done.5 = bf16[64,1664]{1,0:T(8,128)(2,1)S(1)} collective-permute-done((bf16[64,1664]{1,0:T(8,128)(2,1)S(1)}, bf16[64,1664]{1,0:T(8,128)(2,1)S(1)}, u32[]{:S(2)}, u32[]{:S(2)}) %collective-permute-start.5) | collective-permute-done | bytes 213024 | tf_op jit(solution)/shard_map/ppermute | solution.py:82
  442.1 6.5 %collective-permute-done.6 = bf16[64,1664]{1,0:T(8,128)(2,1)S(1)} collective-permute-done((bf16[64,1664]{1,0:T(8,128)(2,1)S(1)}, bf16[64,1664]{1,0:T(8,128)(2,1)S(1)}, u32[]{:S(2)}, u32[]{:S(2)}) %collective-permute-start.6) | collective-permute-done | bytes 213024 | tf_op jit(solution)/shard_map/ppermute | solution.py:82
  449.4 34.3 %all-gather.9.cloned.1.call-done = bf16[4,208,1664]{1,0,2:T(4,128)(2,1)} async-done(((bf16[4,208,52]{1,0,2:T(4,128)(2,1)}), bf16[4,208,1664]{1,0,2:T(4,128)(2,1)}) %all-gather.9.cloned.1.call-update) | async-done | bytes 2768912 | tf_op jit(solution)/shard_map/all_gather | solution.py:20
  483.6 3.8 fusion.23
  487.9 30.3 %reduce-scatter.7.cloned.1.call-done = bf16[208,128]{1,0:T(8,128)(2,1)} async-done(((bf16[1664,128]{1,0:T(8,128)(2,1)}), bf16[208,128]{1,0:T(8,128)(2,1)}) %reduce-scatter.7.cloned.1.call-update) | async-done | bytes 53264
  519.3 19.5 %all_to_all.5 = bf16[32,8,208]{2,1,0:T(8,128)(2,1)S(1)} all-to-all(bf16[32,8,208]{2,1,0:T(8,128)(2,1)S(1)} %bitcast.71), channel_id=1, replica_groups=mesh['wide'=32,'narrow'=8] {'wide'}, dimensions={0} | all-to-all | bytes 212992 | tf_op jit(solution)/shard_map/all_to_all | solution.py:110
  (475 shorter events, 168.1 us)
Async XLA Ops:
  7.2 58.8 %copy-start.2 = (bf16[208,52]{0,1:T(8,128)(2,1)S(1)}, bf16[208,52]{0,1:T(8,128)(2,1)}, u32[]{:S(2)}) copy-start(bf16[208,52]{0,1:T(8,128)(2,1)} %param.14) | copy-start | bytes 64900
  7.2 109.1 %all-gather.5.cloned.1.call-start = ((), (), s32[]{:S(2)}) async-start(), calls=%async_computation.3 | async-start | bytes 7028736 | tf_op jit(solution)/shard_map/all_gather | solution.py:52
  7.9 190.4 %all-gather.7.cloned.1.call-start = ((), (), s32[]{:S(2)}) async-start(), calls=%async_computation.4 | async-start | bytes 7028736 | tf_op jit(solution)/shard_map/all_gather | solution.py:53
  8.7 393.6 %reduce-scatter.5.cloned.1.call-start = ((), (), s32[]{:S(2)}) async-start(), calls=%async_computation.5 | async-start | bytes 1916928 | tf_op jit(solution)/shard_map/reduce_scatter | solution.py:75
  365.6 36.6 %copy-start.1 = (bf16[64,1664]{1,0:T(8,128)(2,1)S(1)}, bf16[64,1664]{1,0:T(8,128)(2,1)}, u32[]{:S(2)}) copy-start(bf16[64,1664]{1,0:T(8,128)(2,1)} %param.10) | copy-start | bytes 638980
  368.8 114.8 %all-gather.9.cloned.1.call-start = ((), (), s32[]{:S(2)}) async-start(), calls=%async_computation.6 | async-start | bytes 3514368 | tf_op jit(solution)/shard_map/all_gather | solution.py:20
  369.4 148.8 %reduce-scatter.7.cloned.1.call-start = ((), (), s32[]{:S(2)}) async-start(), calls=%async_computation.7 | async-start | bytes 479232
  403.2 45.9 %copy-start = (bf16[64,1664]{1,0:T(8,128)(2,1)}, bf16[64,1664]{1,0:T(8,128)(2,1)S(1)}, u32[]{:S(2)}) copy-start(bf16[64,1664]{1,0:T(8,128)(2,1)S(1)} %add_convert_fusion) | copy-start | bytes 638980
  403.2 6.5 %collective-permute-start = (bf16[64,1664]{1,0:T(8,128)(2,1)S(1)}, bf16[64,1664]{1,0:T(8,128)(2,1)S(1)}, u32[]{:S(2)}, u32[]{:S(2)}) collective-permute-start(bf16[64,1664]{1,0:T(8,128)(2,1)S(1)} %add_convert_fusion), channel_id=1, source_target_pairs={{0,1},{1,2},{2,3},{3,4},{4,5},{5,6},{6,7},{7,0},{8,9},{9,10},{10,1... | collective-permute-start | bytes 638984 | tf_op jit(solution)/shard_map/ppermute | solution.py:82
  409.7 6.5 %collective-permute-start.1 = (bf16[64,1664]{1,0:T(8,128)(2,1)S(1)}, bf16[64,1664]{1,0:T(8,128)(2,1)S(1)}, u32[]{:S(2)}, u32[]{:S(2)}) collective-permute-start(bf16[64,1664]{1,0:T(8,128)(2,1)S(1)} %collective-permute-done), channel_id=1, source_target_pairs={{0,1},{1,2},{2,3},{3,4},{4,5},{5,6},{6,7},{7,0},{8,9},{9,10},{10,1... | collective-permute-start | bytes 638984 | tf_op jit(solution)/shard_map/ppermute | solution.py:82
  416.2 6.5 %collective-permute-start.2 = (bf16[64,1664]{1,0:T(8,128)(2,1)S(1)}, bf16[64,1664]{1,0:T(8,128)(2,1)S(1)}, u32[]{:S(2)}, u32[]{:S(2)}) collective-permute-start(bf16[64,1664]{1,0:T(8,128)(2,1)S(1)} %collective-permute-done.1), channel_id=1, source_target_pairs={{0,1},{1,2},{2,3},{3,4},{4,5},{5,6},{6,7},{7,0},{8,9},{9,10},{10,1... | collective-permute-start | bytes 638984 | tf_op jit(solution)/shard_map/ppermute | solution.py:82
  422.7 6.5 %collective-permute-start.3 = (bf16[64,1664]{1,0:T(8,128)(2,1)S(1)}, bf16[64,1664]{1,0:T(8,128)(2,1)S(1)}, u32[]{:S(2)}, u32[]{:S(2)}) collective-permute-start(bf16[64,1664]{1,0:T(8,128)(2,1)S(1)} %collective-permute-done.2), channel_id=1, source_target_pairs={{0,1},{1,2},{2,3},{3,4},{4,5},{5,6},{6,7},{7,0},{8,9},{9,10},{10,1... | collective-permute-start | bytes 638984 | tf_op jit(solution)/shard_map/ppermute | solution.py:82
  429.2 6.5 %collective-permute-start.4 = (bf16[64,1664]{1,0:T(8,128)(2,1)S(1)}, bf16[64,1664]{1,0:T(8,128)(2,1)S(1)}, u32[]{:S(2)}, u32[]{:S(2)}) collective-permute-start(bf16[64,1664]{1,0:T(8,128)(2,1)S(1)} %collective-permute-done.3), channel_id=1, source_target_pairs={{0,1},{1,2},{2,3},{3,4},{4,5},{5,6},{6,7},{7,0},{8,9},{9,10},{10,1... | collective-permute-start | bytes 638984 | tf_op jit(solution)/shard_map/ppermute | solution.py:82
  435.7 6.5 %collective-permute-start.5 = (bf16[64,1664]{1,0:T(8,128)(2,1)S(1)}, bf16[64,1664]{1,0:T(8,128)(2,1)S(1)}, u32[]{:S(2)}, u32[]{:S(2)}) collective-permute-start(bf16[64,1664]{1,0:T(8,128)(2,1)S(1)} %collective-permute-done.4), channel_id=1, source_target_pairs={{0,1},{1,2},{2,3},{3,4},{4,5},{5,6},{6,7},{7,0},{8,9},{9,10},{10,1... | collective-permute-start | bytes 638984 | tf_op jit(solution)/shard_map/ppermute | solution.py:82
  442.1 6.5 %collective-permute-start.6 = (bf16[64,1664]{1,0:T(8,128)(2,1)S(1)}, bf16[64,1664]{1,0:T(8,128)(2,1)S(1)}, u32[]{:S(2)}, u32[]{:S(2)}) collective-permute-start(bf16[64,1664]{1,0:T(8,128)(2,1)S(1)} %collective-permute-done.5), channel_id=1, source_target_pairs={{0,1},{1,2},{2,3},{3,4},{4,5},{5,6},{6,7},{7,0},{8,9},{9,10},{10,1... | collective-permute-start | bytes 638984 | tf_op jit(solution)/shard_map/ppermute | solution.py:82
  449.0 38.4 %copy-start.3 = (s32[128,1]{0,1:T(1,128)S(1)}, s32[128,1]{0,1:T(1,128)}, u32[]{:S(2)}) copy-start(s32[128,1]{0,1:T(1,128)} %param.17) | copy-start | bytes 1540
Sparse Core Ops, SparseCore 0:
  10.6 96.2 all-gather.4
  109.5 88.7 all-gather.6
  369.0 33.2 reduce-scatter.4
  405.0 78.5 all-gather.8
  487.6 30.6 reduce-scatter.6
